TPU v7x, 128 devices: a whole 4x4x4 slice. The times are simulated.
128 devices in a mesh: dp: 16 (over x, z), tensor: 8 (over y, core).
Axes of the slice: x: 4, y: 4, z: 4, core: 2. Of those that a mesh axis runs over, the one named last changes fastest.
Arguments:
- attn_norm_grad: bfloat16 [16, 2048], P('dp', 'tensor'), may hold values from -1.5 to 1.5
- query_grad: bfloat16 [16, 2048, 2048], P('dp', None, 'tensor'), may hold values from -1.5 to 1.5
- forget_grad: bfloat16 [16, 2048, 2048], P('dp', None, 'tensor'), may hold values from -1.5 to 1.5
- input_grad: bfloat16 [16, 2048, 2048], P('dp', None, 'tensor'), may hold values from -1.5 to 1.5
- group_norm_grad: bfloat16 [16, 2048], P('dp', 'tensor'), may hold values from -1.5 to 1.5
- output_gate_grad: bfloat16 [16, 2048, 2048], P('dp', None, 'tensor'), may hold values from -1.5 to 1.5
- out_proj_grad: bfloat16 [16, 2048, 2048], P('dp', 'tensor'), may hold values from -1.5 to 1.5
- mlp_norm_grad: bfloat16 [16, 2048], P('dp', 'tensor'), may hold values from -1.5 to 1.5
- gate_proj_grad: bfloat16 [16, 2048, 2816], P('dp', None, 'tensor'), may hold values from -1.5 to 1.5
- up_proj_grad: bfloat16 [16, 2048, 2816], P('dp', None, 'tensor'), may hold values from -1.5 to 1.5
- down_proj_grad: bfloat16 [16, 2816, 2048], P('dp', 'tensor'), may hold values from -1.5 to 1.5
- weights: float32 [8, 4784896], P('tensor', 'dp'), as said below
- first_moment: float32 [8, 4784896], P('tensor', 'dp'), may hold values from -0.6 to 0.6
- second_moment: float32 [8, 4784896], P('tensor', 'dp'), may hold values from 0.001 to 1
Outputs:
- new_weights: float32 [8, 4784896], P('tensor', 'dp')
- new_first: float32 [8, 4784896], P('tensor', 'dp')
- new_second: float32 [8, 4784896], P('tensor', 'dp')
- attn_norm_copy: bfloat16 [2048], P('tensor')
- query_copy: bfloat16 [2048, 2048], P(None, 'tensor')
- forget_copy: bfloat16 [2048, 2048], P(None, 'tensor')
- input_copy: bfloat16 [2048, 2048], P(None, 'tensor')
- group_norm_copy: bfloat16 [2048], P('tensor')
- output_gate_copy: bfloat16 [2048, 2048], P(None, 'tensor')
- out_proj_copy: bfloat16 [2048, 2048], P('tensor')
- mlp_norm_copy: bfloat16 [2048], P('tensor')
- gate_proj_copy: bfloat16 [2048, 2816], P(None, 'tensor')
- up_proj_copy: bfloat16 [2048, 2816], P(None, 'tensor')
- down_proj_copy: bfloat16 [2816, 2048], P('tensor')
Inputs may be any that keep to these rules, and one draw needn't show every extreme that they name: float32 master weights of order one.
All inputs are finite; a program needn't handle non-finite values.
Results may differ from a plain program's by a relative error of at most 0.0085.
Values may be sent and summed in bfloat16 or wider, within the bound.
A program may use at most 192 MiB of HBM per device.

v0:
```python
import jax
import jax.numpy as jnp
from jax import lax
from jax.sharding import PartitionSpec as P

GAIN_SEGMENTS = (0, 4, 7)


def segment_sums(onehot, values):
    return jnp.dot(onehot, values, precision=lax.Precision.HIGHEST)


def split_rows(block, owners):
    if block.ndim == 1:
        return block.reshape(owners, block.shape[0] // owners)
    return block.reshape(owners, block.shape[0] // owners, block.shape[1])


def on_device(
    attn_norm_grad,
    query_grad,
    forget_grad,
    input_grad,
    group_norm_grad,
    output_gate_grad,
    out_proj_grad,
    mlp_norm_grad,
    gate_proj_grad,
    up_proj_grad,
    down_proj_grad,
    weights,
    first_moment,
    second_moment,
):
    grads = (
        attn_norm_grad,
        query_grad,
        forget_grad,
        input_grad,
        group_norm_grad,
        output_gate_grad,
        out_proj_grad,
        mlp_norm_grad,
        gate_proj_grad,
        up_proj_grad,
        down_proj_grad,
    )
    owners = lax.axis_size("dp")
    shapes = [g.shape[1:] for g in grads]
    pieces = [split_rows(g[0], owners) for g in grads]
    piece_len = [p[0].size for p in pieces]
    own_count = sum(piece_len)
    weight_row = weights.reshape(-1)
    first_row = first_moment.reshape(-1)
    second_row = second_moment.reshape(-1)
    position = jnp.arange(own_count, dtype=jnp.int32)
    segment = jnp.zeros((own_count,), jnp.int32)
    bound = 0
    for number in range(10):
        bound += piece_len[number]
        segment = segment + (position >= bound).astype(jnp.int32)
    onehot = (segment[None, :] == jnp.arange(11, dtype=jnp.int32)[:, None]).astype(jnp.float32)
    gain_mask = onehot[GAIN_SEGMENTS[0]] + onehot[GAIN_SEGMENTS[1]] + onehot[GAIN_SEGMENTS[2]]
    summed = (
        lax.psum_scatter(
            pieces[0].astype(jnp.float32).astype(jnp.bfloat16),
            "dp",
            scatter_dimension=0,
            tiled=True,
        ).astype(jnp.float32),
        lax.psum_scatter(
            pieces[1].astype(jnp.float32).astype(jnp.bfloat16),
            "dp",
            scatter_dimension=0,
            tiled=True,
        ).astype(jnp.float32),
        lax.psum_scatter(
            pieces[2].astype(jnp.float32).astype(jnp.bfloat16),
            "dp",
            scatter_dimension=0,
            tiled=True,
        ).astype(jnp.float32),
        lax.psum_scatter(
            pieces[3].astype(jnp.float32).astype(jnp.bfloat16),
            "dp",
            scatter_dimension=0,
            tiled=True,
        ).astype(jnp.float32),
        lax.psum_scatter(
            pieces[4].astype(jnp.float32).astype(jnp.bfloat16),
            "dp",
            scatter_dimension=0,
            tiled=True,
        ).astype(jnp.float32),
        lax.psum_scatter(
            pieces[5].astype(jnp.float32).astype(jnp.bfloat16),
            "dp",
            scatter_dimension=0,
            tiled=True,
        ).astype(jnp.float32),
        lax.psum_scatter(
            pieces[6].astype(jnp.float32).astype(jnp.bfloat16),
            "dp",
            scatter_dimension=0,
            tiled=True,
        ).astype(jnp.float32),
        lax.psum_scatter(
            pieces[7].astype(jnp.float32).astype(jnp.bfloat16),
            "dp",
            scatter_dimension=0,
            tiled=True,
        ).astype(jnp.float32),
        lax.psum_scatter(
            pieces[8].astype(jnp.float32).astype(jnp.bfloat16),
            "dp",
            scatter_dimension=0,
            tiled=True,
        ).astype(jnp.float32),
        lax.psum_scatter(
            pieces[9].astype(jnp.float32).astype(jnp.bfloat16),
            "dp",
            scatter_dimension=0,
            tiled=True,
        ).astype(jnp.float32),
        lax.psum_scatter(
            pieces[10].astype(jnp.float32).astype(jnp.bfloat16),
            "dp",
            scatter_dimension=0,
            tiled=True,
        ).astype(jnp.float32),
    )
    grad = jnp.concatenate([s.reshape(-1) for s in summed])
    new_first = 0.9 * first_row + 0.1 * grad
    new_second = 0.999 * second_row + 0.001 * grad * grad
    update = new_first / (jnp.sqrt(new_second) + 1e-06) + 0.01 * weight_row * (1.0 - gain_mask)
    weight_sq, update_sq = lax.psum(
        (segment_sums(onehot, weight_row * weight_row), segment_sums(onehot, update * update)),
        ("dp", "tensor"),
    )
    trust = jnp.sqrt(weight_sq) / jnp.sqrt(update_sq)
    scale = jnp.dot(trust, onehot, precision=lax.Precision.HIGHEST)
    new_weights = weight_row - 0.1 * scale * update
    rounded = new_weights.astype(jnp.bfloat16)
    owned = []
    offset = 0
    for number in range(11):
        owned.append(
            rounded[offset : offset + piece_len[number]].reshape((1,) + pieces[number].shape[1:])
        )
        offset += piece_len[number]
    gathered = (
        lax.all_gather(owned[0], "dp", axis=0, tiled=True),
        lax.all_gather(owned[1], "dp", axis=0, tiled=True),
        lax.all_gather(owned[2], "dp", axis=0, tiled=True),
        lax.all_gather(owned[3], "dp", axis=0, tiled=True),
        lax.all_gather(owned[4], "dp", axis=0, tiled=True),
        lax.all_gather(owned[5], "dp", axis=0, tiled=True),
        lax.all_gather(owned[6], "dp", axis=0, tiled=True),
        lax.all_gather(owned[7], "dp", axis=0, tiled=True),
        lax.all_gather(owned[8], "dp", axis=0, tiled=True),
        lax.all_gather(owned[9], "dp", axis=0, tiled=True),
        lax.all_gather(owned[10], "dp", axis=0, tiled=True),
    )
    copies = [gathered[number].reshape(shapes[number]) for number in range(11)]
    return (
        new_weights.reshape(1, -1),
        new_first.reshape(1, -1),
        new_second.reshape(1, -1),
        copies[0],
        copies[1],
        copies[2],
        copies[3],
        copies[4],
        copies[5],
        copies[6],
        copies[7],
        copies[8],
        copies[9],
        copies[10],
    )


def solution(mesh):
    return jax.shard_map(
        on_device,
        mesh=mesh,
        in_specs=(
            P("dp", "tensor"),
            P("dp", None, "tensor"),
            P("dp", None, "tensor"),
            P("dp", None, "tensor"),
            P("dp", "tensor"),
            P("dp", None, "tensor"),
            P("dp", "tensor", None),
            P("dp", "tensor"),
            P("dp", None, "tensor"),
            P("dp", None, "tensor"),
            P("dp", "tensor", None),
            P("tensor", "dp"),
            P("tensor", "dp"),
            P("tensor", "dp"),
        ),
        out_specs=(
            P("tensor", "dp"),
            P("tensor", "dp"),
            P("tensor", "dp"),
            P("tensor"),
            P(None, "tensor"),
            P(None, "tensor"),
            P(None, "tensor"),
            P("tensor"),
            P(None, "tensor"),
            P("tensor", None),
            P("tensor"),
            P(None, "tensor"),
            P(None, "tensor"),
            P("tensor", None),
        ),
        check_vma=False,
    )
```

profile of v0, /device:TPU:0, one launch (start us, length us, event | category | flops | bytes accessed | tf_op | source)
XLA Modules:
  0.0 1172.6 jit_solution(3635013927501478566)
XLA Ops:
  11.1 1.5 copy.40
  12.7 1.3 copy-done.2
  14.3 1.5 copy.42
  15.9 1.3 copy-done.3
  17.2 1.4 reshape_squeeze.43
  18.8 8.6 fusion.2
  27.7 13.4 %reduce = f32[299056]{0:T(1024)S(1)} reduce(f32[1,299056]{1,0:T(1,128)} %param.25, f32[]{:T(128)} %constant.110), dimensions={0}, to_apply=%param.25.reduce_sub_computation | reduce | bytes 2392452 | tf_op args[11]
  41.1 76.1 %all-reduce.16 = (bf16[16,16]{1,0:T(8,128)(2,1)S(1)}, bf16[16,16]{1,0:T(8,128)(2,1)S(1)}, bf16[16,16]{1,0:T(8,128)(2,1)S(1)}) all-reduce(bf16[16,16]{1,0:T(8,128)(2,1)S(1)} %reshape_squeeze.33, bf16[16,16]{1,0:T(8,128)(2,1)S(1)} %reshape_squeeze.37, ...), channel_id=5, replica_groups=mesh['dp'=16,'tensor'=8] {'dp'}, use_global_device_ids=true, to_apply=%region_1.0.clone | all-reduce | flops 768 | bytes 3072
  119.1 1.2 dynamic-update-slice.3
  121.0 20.0 %fusion.15 = f32[299056]{0:T(1024)} fusion(f32[11,299056]{1,0:T(8,128)} %fusion.2), kind=kLoop, calls=%fused_computation.35 | loop fusion | flops 897168 | bytes 4784896 | tf_op jit(solution)/shard_map/sub | solution.py:135
  141.0 0.9 convert_bitcast_fusion.8
  142.1 20.7 %reduce-scatter.27.cloned.1.call-done = bf16[1,128,256]{2,1,0:T(8,128)(2,1)} async-done(((bf16[16,128,256]{2,1,0:T(8,128)(2,1)}), bf16[1,128,256]{2,1,0:T(8,128)(2,1)}) %reduce-scatter.27.cloned.1.call-update) | async-done | bytes 65552
  162.7 0.9 convert_bitcast_fusion.6
  163.7 74.5 %reduce-scatter.29.cloned.1.call-done = bf16[1,128,256]{2,1,0:T(8,128)(2,1)} async-done(((bf16[16,128,256]{2,1,0:T(8,128)(2,1)}), bf16[1,128,256]{2,1,0:T(8,128)(2,1)}) %reduce-scatter.29.cloned.1.call-update) | async-done | bytes 65552
  238.3 1.5 convert_bitcast_fusion.4
  239.9 74.0 %reduce-scatter.31.cloned.1.call-done = bf16[1,128,256]{2,1,0:T(8,128)(2,1)} async-done(((bf16[16,128,256]{2,1,0:T(8,128)(2,1)}), bf16[1,128,256]{2,1,0:T(8,128)(2,1)}) %reduce-scatter.31.cloned.1.call-update) | async-done | bytes 65552
  313.9 1.5 convert_bitcast_fusion.2
  315.6 73.7 %reduce-scatter.33.cloned.1.call-done = bf16[1,16,2048]{2,1,0:T(8,128)(2,1)} async-done(((bf16[16,16,2048]{2,1,0:T(8,128)(2,1)}), bf16[1,16,2048]{2,1,0:T(8,128)(2,1)}) %reduce-scatter.33.cloned.1.call-update) | async-done | bytes 65552
  389.3 0.9 convert_bitcast_fusion
  390.5 0.7 copy.53
  393.3 3.8 dynamic-update-slice.4
  397.1 3.8 dynamic-update-slice.5
  400.8 3.8 dynamic-update-slice.6
  404.6 1.4 dynamic-update-slice.7
  405.9 3.8 dynamic-update-slice.8
  409.7 3.8 dynamic-update-slice.9
  413.5 1.4 dynamic-update-slice.10
  414.8 51.4 %reduce-scatter.35.cloned.1.call-done = bf16[1,128,352]{1,2,0:T(8,128)(2,1)} async-done(((bf16[16,128,352]{1,2,0:T(8,128)(2,1)}), bf16[1,128,352]{1,2,0:T(8,128)(2,1)}) %reduce-scatter.35.cloned.1.call-update) | async-done | bytes 90128
  466.2 1.0 copy.41
  467.7 75.6 %reduce-scatter.37.cloned.1.call-done = bf16[1,128,352]{1,2,0:T(8,128)(2,1)} async-done(((bf16[16,128,352]{1,2,0:T(8,128)(2,1)}), bf16[1,128,352]{1,2,0:T(8,128)(2,1)}) %reduce-scatter.37.cloned.1.call-update) | async-done | bytes 90128
  543.3 1.0 copy.43
  544.8 75.0 %reduce-scatter.39.cloned.1.call-done = bf16[1,22,2048]{2,1,0:T(8,128)(2,1)} async-done(((bf16[16,22,2048]{2,1,0:T(8,128)(2,1)}), bf16[1,22,2048]{2,1,0:T(8,128)(2,1)}) %reduce-scatter.39.cloned.1.call-update) | async-done | bytes 90128
  619.8 0.9 convert_bitcast_fusion.10
  620.9 4.4 dynamic-update-slice.11
  625.3 4.4 dynamic-update-slice.12
  629.6 4.3 dynamic-update-slice.13
  634.0 21.6 %fusion.13 = (f32[1,299056]{1,0:T(1,128)}, f32[299056]{0:T(1024)}, f32[1,299056]{1,0:T(1,128)}, f32[299056]{0:T(1024)}) fusion(f32[1,299056]{1,0:T(1,128)} %dynamic-update-slice.13, f32[1,299056]{1,0:T(1,128)} %param.27, f32[1,299056]{1,0:T(1,128)} %param.26), kind=kLoop, calls=%fused_computation.30 | loop fusion | flops 2093392 | bytes 8373568 | tf_op jit(solution)/shard_map/add | solution.py:134
  655.7 16.2 %concatenate.41 = f32[299056]{0:T(1024)} concatenate(f32[16]{0:T(128)S(1)} %bitcast.103, f32[32768]{0:T(1024)S(1)} %bitcast.93, f32[32768]{0:T(1024)S(1)} %bitcast.94, f32[32768]{0:T(1024)S(1)} %bitcast.95, f32[16]{0:T(128)S(1)} %fusion.32, f32[32768]{0:T(1024)} %bitcast.96, f32[32768]{0:T(1024)} %bitcast.97, f32[16]{0:T(128)S(1)} %bitcast.104, f32[45056]{0:T(1024)S(1)} %reshape.617, ...), dimensions={0} | concatenate | bytes 2392448 | tf_op jit(solution)/shard_map/concatenate | solution.py:132
  671.9 4.2 fusion.24
  676.1 5.7 reshape.666
  681.8 12.5 %fusion.17 = f32[11]{0:T(128)S(1)} fusion(f32[299056,1]{0,1:T(1,128)S(1)} %reshape.666, s32[299056]{0:T(1024)S(1)} %convert_add_fusion), kind=kOutput, calls=%fused_computation.37 | convolution fusion | flops 42765008 | bytes 2392492 | tf_op jit(solution)/shard_map/dot_general | solution.py:10
  694.3 5.8 reshape.664
  700.1 12.5 %fusion.16 = f32[11]{0:T(128)S(1)} fusion(f32[299056,1]{0,1:T(1,128)S(1)} %reshape.664, s32[299056]{0:T(1024)S(1)} %convert_add_fusion), kind=kOutput, calls=%fused_computation.36 | convolution fusion | flops 42765008 | bytes 2392492 | tf_op jit(solution)/shard_map/dot_general | solution.py:10
  712.6 65.0 %all-reduce.14 = (f32[11]{0:T(128)S(1)}, f32[11]{0:T(128)S(1)}) all-reduce(f32[11]{0:T(128)S(1)} %fusion.17, f32[11]{0:T(128)S(1)} %fusion.16), channel_id=1, replica_groups=mesh['dp'=16,'tensor'=8] {'dp','tensor'}, use_global_device_ids=true, to_apply=%region_12.0 | all-reduce | flops 22 | bytes 176 | tf_op jit(solution)/shard_map/psum | solution.py:136
  777.6 20.0 %fusion.7 = f32[299056]{0:T(1024)S(1)} fusion(s32[299056]{0:T(1024)S(1)} %convert_add_fusion, f32[11]{0:T(128)S(1)} %get-tuple-element.28, f32[11]{0:T(128)S(1)} %get-tuple-element.29), kind=kOutput, calls=%fused_computation.22 | convolution fusion | flops 42765020 | bytes 2392536 | tf_op jit(solution)/shard_map/dot_general | solution.py:141
  802.0 0.7 copy.46
  803.0 0.7 copy.48
  805.2 6.5 reshape.620
  812.4 38.4 %all-reduce.15 = (bf16[256]{0:T(256)(128)(2,1)}, bf16[256]{0:T(256)(128)(2,1)}, bf16[256]{0:T(256)(128)(2,1)}) all-reduce(bf16[256]{0:T(256)(128)(2,1)S(1)} %dynamic-update-slice, bf16[256]{0:T(256)(128)(2,1)S(1)} %dynamic-update-slice.1, bf16[256]{0:T(256)(128)(2,1)S(1)} %dynamic-update-slice.2), channel_id=2, replica_groups=mesh['dp'=16,'tensor'=8] {'dp'}, use_global_device_ids=true, to_apply=%add | all-reduce | flops 768 | bytes 3072
  850.8 31.7 %all-gather.14.cloned.1.call-done = bf16[16,128,256]{2,1,0:T(8,128)(2,1)} async-done(((bf16[1,128,256]{2,1,0:T(8,128)(2,1)}), bf16[16,128,256]{2,1,0:T(8,128)(2,1)}) %all-gather.14.cloned.1.call-update) | async-done | bytes 1048592 | tf_op jit(solution)/shard_map/all_gather | solution.py:154
  882.5 45.1 %all-gather.16.cloned.1.call-done = bf16[16,128,256]{2,1,0:T(8,128)(2,1)} async-done(((bf16[1,128,256]{2,1,0:T(8,128)(2,1)}), bf16[16,128,256]{2,1,0:T(8,128)(2,1)}) %all-gather.16.cloned.1.call-update) | async-done | bytes 1048592 | tf_op jit(solution)/shard_map/all_gather | solution.py:155
  927.6 44.9 %all-gather.18.cloned.1.call-done = bf16[16,128,256]{2,1,0:T(8,128)(2,1)} async-done(((bf16[1,128,256]{2,1,0:T(8,128)(2,1)}), bf16[16,128,256]{2,1,0:T(8,128)(2,1)}) %all-gather.18.cloned.1.call-update) | async-done | bytes 1048592 | tf_op jit(solution)/shard_map/all_gather | solution.py:157
  972.5 45.1 %all-gather.20.cloned.1.call-done = bf16[16,16,2048]{2,1,0:T(8,128)(2,1)} async-done(((bf16[1,16,2048]{2,1,0:T(8,128)(2,1)}), bf16[16,16,2048]{2,1,0:T(8,128)(2,1)}) %all-gather.20.cloned.1.call-update) | async-done | bytes 1048592 | tf_op jit(solution)/shard_map/all_gather | solution.py:158
  1017.6 46.1 %all-gather.22.cloned.1.call-done = bf16[16,128,352]{1,2,0:T(8,128)(2,1)} async-done(((bf16[1,128,352]{1,2,0:T(8,128)(2,1)}), bf16[16,128,352]{1,2,0:T(8,128)(2,1)}) %all-gather.22.cloned.1.call-update) | async-done | bytes 1441808 | tf_op jit(solution)/shard_map/all_gather | solution.py:160
  1063.7 2.6 copy_bitcast_fusion.1
  1066.3 43.5 %all-gather.24.cloned.1.call-done = bf16[16,128,352]{1,2,0:T(8,128)(2,1)} async-done(((bf16[1,128,352]{1,2,0:T(8,128)(2,1)}), bf16[16,128,352]{1,2,0:T(8,128)(2,1)}) %all-gather.24.cloned.1.call-update) | async-done | bytes 1441808 | tf_op jit(solution)/shard_map/all_gather | solution.py:161
  1109.8 2.6 copy_bitcast_fusion
  1112.4 43.6 %all-gather.26.cloned.1.call-done = bf16[16,22,2048]{2,1,0:T(8,128)(2,1)} async-done(((bf16[1,22,2048]{2,1,0:T(8,128)(2,1)}), bf16[16,22,2048]{2,1,0:T(8,128)(2,1)}) %all-gather.26.cloned.1.call-update) | async-done | bytes 1441808 | tf_op jit(solution)/shard_map/all_gather | solution.py:162
  1156.0 2.4 reshape.642
  1158.5 1.0 copy.86
  1160.1 1.0 copy.87
  1161.7 1.0 copy.88
  1163.3 1.0 copy.89
  1164.9 1.0 copy.90
  (115 shorter events, 19.9 us)
Async XLA Ops:
  7.2 133.9 %reduce-scatter.25.cloned.1.call-start = ((), (), s32[]{:S(2)}) async-start(), calls=%async_computation.16 | async-start | bytes 1114112
  7.9 154.8 %reduce-scatter.27.cloned.1.call-start = ((), (), s32[]{:S(2)}) async-start(), calls=%async_computation.17 | async-start | bytes 1114112
  8.7 229.6 %reduce-scatter.29.cloned.1.call-start = ((), (), s32[]{:S(2)}) async-start(), calls=%async_computation.18 | async-start | bytes 1114112
  9.4 1.4 copy-start.1
  9.4 304.5 %reduce-scatter.31.cloned.1.call-start = ((), (), s32[]{:S(2)}) async-start(), calls=%async_computation.19 | async-start | bytes 1114112
  10.0 379.3 %reduce-scatter.33.cloned.1.call-start = ((), (), s32[]{:S(2)}) async-start(), calls=%async_computation.20 | async-start | bytes 1114112
  10.6 455.7 %reduce-scatter.35.cloned.1.call-start = ((), (), s32[]{:S(2)}) async-start(), calls=%async_computation.21 | async-start | bytes 1531904
  12.6 1.4 copy-start.2
  12.6 530.7 %reduce-scatter.37.cloned.1.call-start = ((), (), s32[]{:S(2)}) async-start(), calls=%async_computation.22 | async-start | bytes 1531904
  15.8 1.4 copy-start.3
  15.8 604.0 %reduce-scatter.39.cloned.1.call-start = ((), (), s32[]{:S(2)}) async-start(), calls=%async_computation.23 | async-start | bytes 1671168
  18.6 832.3 %all-gather.12.cloned.1.call-start = ((), (), s32[]{:S(2)}) async-start(), calls=%async_computation.8 | async-start | bytes 1114112 | tf_op jit(solution)/shard_map/all_gather | solution.py:153
  18.7 8.6 copy-start.15
  18.7 8.7 copy-start.16
  18.7 8.8 copy-start.17
  27.7 89.5 %copy-start.14 = (u32[128]{0:T(128)S(1)}, u32[128]{0:T(128)}, u32[]{:S(2)}) copy-start(u32[128]{0:T(128)} %constant.50) | copy-start | bytes 1540
  389.3 1.9 copy-start.11
  389.3 2.6 copy-start.12
  633.9 21.6 %copy-start.13 = (bf16[1,22,2048]{2,1,0:T(8,128)(2,1)S(1)}, bf16[1,22,2048]{2,1,0:T(8,128)(2,1)}, u32[]{:S(2)}) copy-start(bf16[1,22,2048]{2,1,0:T(8,128)(2,1)} %reduce-scatter.39.cloned.1.call-done) | copy-start | bytes 270340
  633.9 21.7 %copy-start.9 = (f32[16,2,8,128]{3,1,2,0:T(2,128)S(1)}, f32[16,2,8,128]{3,1,2,0:T(2,128)}, u32[]{:S(2)}) copy-start(f32[16,2,8,128]{3,1,2,0:T(2,128)} %copy.53) | copy-start | bytes 393220
  634.0 21.7 %copy-start.10 = (f32[16,2,8,128]{3,1,2,0:T(2,128)S(1)}, f32[16,2,8,128]{3,1,2,0:T(2,128)}, u32[]{:S(2)}) copy-start(f32[16,2,8,128]{3,1,2,0:T(2,128)} %copy.54) | copy-start | bytes 393220
  777.6 20.0 %copy-start = (f32[299056]{0:T(1024)S(1)}, f32[299056]{0:T(1024)}, u32[]{:S(2)}) copy-start(f32[299056]{0:T(1024)} %get-tuple-element.39) | copy-start | bytes 3588676
  798.7 83.8 %all-gather.14.cloned.1.call-start = ((), (), s32[]{:S(2)}) async-start(), calls=%async_computation.9 | async-start | bytes 1114112 | tf_op jit(solution)/shard_map/all_gather | solution.py:154
  799.5 128.2 %all-gather.16.cloned.1.call-start = ((), (), s32[]{:S(2)}) async-start(), calls=%async_computation.10 | async-start | bytes 1114112 | tf_op jit(solution)/shard_map/all_gather | solution.py:155
  800.2 172.3 %all-gather.18.cloned.1.call-start = ((), (), s32[]{:S(2)}) async-start(), calls=%async_computation.11 | async-start | bytes 1114112 | tf_op jit(solution)/shard_map/all_gather | solution.py:157
  800.9 216.7 %all-gather.20.cloned.1.call-start = ((), (), s32[]{:S(2)}) async-start(), calls=%async_computation.12 | async-start | bytes 1114112 | tf_op jit(solution)/shard_map/all_gather | solution.py:158
  801.7 262.0 %all-gather.22.cloned.1.call-start = ((), (), s32[]{:S(2)}) async-start(), calls=%async_computation.13 | async-start | bytes 1531904 | tf_op jit(solution)/shard_map/all_gather | solution.py:160
  802.8 307.0 %all-gather.24.cloned.1.call-start = ((), (), s32[]{:S(2)}) async-start(), calls=%async_computation.14 | async-start | bytes 1531904 | tf_op jit(solution)/shard_map/all_gather | solution.py:161
  803.8 352.2 %all-gather.26.cloned.1.call-start = ((), (), s32[]{:S(2)}) async-start(), calls=%async_computation.15 | async-start | bytes 1671168 | tf_op jit(solution)/shard_map/all_gather | solution.py:162
  1112.4 46.0 %copy-start.4 = (bf16[16,128,256]{2,1,0:T(8,128)(2,1)S(1)}, bf16[16,128,256]{2,1,0:T(8,128)(2,1)}, u32[]{:S(2)}) copy-start(bf16[16,128,256]{2,1,0:T(8,128)(2,1)} %all-gather.12.cloned.1.call-done) | copy-start | bytes 3145732
  1158.5 1.6 copy-start.5
  1160.1 1.6 copy-start.6
  1161.7 1.6 copy-start.7
  1163.3 1.6 copy-start.8
Sparse Core Ops, SparseCore 0:
  11.2 75.6 reduce-scatter.24
  90.4 72.2 reduce-scatter.26
  165.9 72.2 reduce-scatter.28
  241.7 72.2 reduce-scatter.30
  317.0 72.2 reduce-scatter.32
  393.3 72.8 reduce-scatter.34
  470.4 72.9 reduce-scatter.36
  546.9 72.9 reduce-scatter.38
  798.8 38.8 all-gather.11
  840.6 41.9 all-gather.13
  885.5 42.0 all-gather.15
  930.4 42.0 all-gather.17
  975.5 42.0 all-gather.19
  1020.5 43.1 all-gather.21
  1066.5 43.2 all-gather.23
  1112.6 43.3 all-gather.25
where the time goes:
time: 1180 us; the launch traced here: 1170 us
  waiting for transfers between devices  748 us (63%)
  blocking collectives  180 us (15%)
  local copies, waits for them, and re-layouts  107 us (9%)
  other arithmetic  76.6 us (6%)
  matrix products  45 us (4%)
  between operations  15.1 us (1%)
    unnamed x24, waiting for transfers between devices  448 us
    unnamed x2, blocking collectives  115 us
    psum x1, blocking collectives, on_device(): lax.psum((segment_sums(onehot, weight_row * weight_row), segment_sums(one...  65 us
    unnamed x71, local copies, waits for them, and re-layouts  47.3 us
    all_gather x1, waiting for transfers between devices, on_device(): lax.all_gather(owned[8], 'dp', axis=0, tiled=True)  46.1 us
    all_gather x1, waiting for transfers between devices, on_device(): lax.all_gather(owned[3], 'dp', axis=0, tiled=True)  45.1 us
    all_gather x1, waiting for transfers between devices, on_device(): lax.all_gather(owned[6], 'dp', axis=0, tiled=True)  45.1 us
    all_gather x1, waiting for transfers between devices, on_device(): lax.all_gather(owned[5], 'dp', axis=0, tiled=True)  44.9 us
  transfers between devices with their start and end apart: 16, of which 14 were waited for; matrix products, arithmetic and copies ran while one was open for 9% of the time, Pallas kernels for 0%

commit v1 on v0

--- a/solution.py
+++ b/solution.py
@@ -134,8 +134,11 @@
     new_second = 0.999 * second_row + 0.001 * grad * grad
     update = new_first / (jnp.sqrt(new_second) + 1e-06) + 0.01 * weight_row * (1.0 - gain_mask)
     weight_sq, update_sq = lax.psum(
-        (segment_sums(onehot, weight_row * weight_row), segment_sums(onehot, update * update)),
-        ("dp", "tensor"),
+        lax.psum(
+            (segment_sums(onehot, weight_row * weight_row), segment_sums(onehot, update * update)),
+            "tensor",
+        ),
+        "dp",
     )
     trust = jnp.sqrt(weight_sq) / jnp.sqrt(update_sq)
     scale = jnp.dot(trust, onehot, precision=lax.Precision.HIGHEST)

time: 1180 us -> 1170 us (level)
  blocking collectives: 180 us -> 164 us
    psum x1, blocking collectives: 65 us -> 13 us  [on_device(): lax.psum((segment_sums(onehot, weight_row * weight_row), segment_sums(one...]
    psum x0 -> x1, blocking collectives: none -> 38.3 us  [on_device(): lax.psum(lax.psum((segment_sums(onehot, weight_row * weight_row), segment...]
where the time goes in v1:
time: 1170 us; the launch traced here: 1160 us
  waiting for transfers between devices  749 us (64%)
  blocking collectives  164 us (14%)
  local copies, waits for them, and re-layouts  107 us (9%)
  other arithmetic  76.4 us (7%)
  matrix products  45 us (4%)
  between operations  15.4 us (1%)
    unnamed x24, waiting for transfers between devices  449 us
    unnamed x2, blocking collectives  112 us
    unnamed x71, local copies, waits for them, and re-layouts  47.3 us
    all_gather x1, waiting for transfers between devices, on_device(): lax.all_gather(owned[8], 'dp', axis=0, tiled=True)  46.1 us
    all_gather x1, waiting for transfers between devices, on_device(): lax.all_gather(owned[3], 'dp', axis=0, tiled=True)  45.1 us
    all_gather x1, waiting for transfers between devices, on_device(): lax.all_gather(owned[6], 'dp', axis=0, tiled=True)  45.1 us
    all_gather x1, waiting for transfers between devices, on_device(): lax.all_gather(owned[5], 'dp', axis=0, tiled=True)  44.9 us
    all_gather x1, waiting for transfers between devices, on_device(): lax.all_gather(owned[10], 'dp', axis=0, tiled=True)  43.6 us
  transfers between devices with their start and end apart: 16, of which 14 were waited for; matrix products, arithmetic and copies ran while one was open for 9% of the time, Pallas kernels for 0%

profile of v1, /device:TPU:0, one launch (start us, length us, event | category | flops | bytes accessed | tf_op | source)
XLA Modules:
  0.0 1157.3 jit_solution(15073703234234142860)
XLA Ops:
  11.1 1.5 copy.40
  12.7 1.3 copy-done.2
  14.3 1.5 copy.42
  15.9 1.3 copy-done.3
  17.2 1.4 reshape_squeeze.43
  18.7 8.6 fusion.2
  27.7 13.4 %reduce = f32[299056]{0:T(1024)S(1)} reduce(f32[1,299056]{1,0:T(1,128)} %param.25, f32[]{:T(128)} %constant.110), dimensions={0}, to_apply=%param.25.reduce_sub_computation | reduce | bytes 2392452 | tf_op args[11]
  41.0 76.1 %all-reduce.17 = (bf16[16,16]{1,0:T(8,128)(2,1)S(1)}, bf16[16,16]{1,0:T(8,128)(2,1)S(1)}, bf16[16,16]{1,0:T(8,128)(2,1)S(1)}) all-reduce(bf16[16,16]{1,0:T(8,128)(2,1)S(1)} %reshape_squeeze.33, bf16[16,16]{1,0:T(8,128)(2,1)S(1)} %reshape_squeeze.37, ...), channel_id=5, replica_groups=mesh['dp'=16,'tensor'=8] {'dp'}, use_global_device_ids=true, to_apply=%region_2.0.clone | all-reduce | flops 768 | bytes 3072
  119.1 1.2 dynamic-update-slice.3
  121.0 20.0 %fusion.15 = f32[299056]{0:T(1024)} fusion(f32[11,299056]{1,0:T(8,128)} %fusion.2), kind=kLoop, calls=%fused_computation.35 | loop fusion | flops 897168 | bytes 4784896 | tf_op jit(solution)/shard_map/sub | solution.py:135
  141.0 0.9 convert_bitcast_fusion.8
  142.0 20.8 %reduce-scatter.27.cloned.1.call-done = bf16[1,128,256]{2,1,0:T(8,128)(2,1)} async-done(((bf16[16,128,256]{2,1,0:T(8,128)(2,1)}), bf16[1,128,256]{2,1,0:T(8,128)(2,1)}) %reduce-scatter.27.cloned.1.call-update) | async-done | bytes 65552
  162.7 0.9 convert_bitcast_fusion.6
  163.7 74.5 %reduce-scatter.29.cloned.1.call-done = bf16[1,128,256]{2,1,0:T(8,128)(2,1)} async-done(((bf16[16,128,256]{2,1,0:T(8,128)(2,1)}), bf16[1,128,256]{2,1,0:T(8,128)(2,1)}) %reduce-scatter.29.cloned.1.call-update) | async-done | bytes 65552
  238.3 1.5 convert_bitcast_fusion.4
  239.9 74.1 %reduce-scatter.31.cloned.1.call-done = bf16[1,128,256]{2,1,0:T(8,128)(2,1)} async-done(((bf16[16,128,256]{2,1,0:T(8,128)(2,1)}), bf16[1,128,256]{2,1,0:T(8,128)(2,1)}) %reduce-scatter.31.cloned.1.call-update) | async-done | bytes 65552
  314.0 1.5 convert_bitcast_fusion.2
  315.6 73.8 %reduce-scatter.33.cloned.1.call-done = bf16[1,16,2048]{2,1,0:T(8,128)(2,1)} async-done(((bf16[16,16,2048]{2,1,0:T(8,128)(2,1)}), bf16[1,16,2048]{2,1,0:T(8,128)(2,1)}) %reduce-scatter.33.cloned.1.call-update) | async-done | bytes 65552
  389.5 0.9 convert_bitcast_fusion
  393.4 3.8 dynamic-update-slice.4
  397.2 3.8 dynamic-update-slice.5
  401.0 3.8 dynamic-update-slice.6
  404.7 1.4 dynamic-update-slice.7
  406.1 3.8 dynamic-update-slice.8
  409.8 3.8 dynamic-update-slice.9
  413.6 1.4 dynamic-update-slice.10
  415.0 51.5 %reduce-scatter.35.cloned.1.call-done = bf16[1,128,352]{1,2,0:T(8,128)(2,1)} async-done(((bf16[16,128,352]{1,2,0:T(8,128)(2,1)}), bf16[1,128,352]{1,2,0:T(8,128)(2,1)}) %reduce-scatter.35.cloned.1.call-update) | async-done | bytes 90128
  466.4 1.0 copy.41
  467.9 75.6 %reduce-scatter.37.cloned.1.call-done = bf16[1,128,352]{1,2,0:T(8,128)(2,1)} async-done(((bf16[16,128,352]{1,2,0:T(8,128)(2,1)}), bf16[1,128,352]{1,2,0:T(8,128)(2,1)}) %reduce-scatter.37.cloned.1.call-update) | async-done | bytes 90128
  543.5 1.0 copy.43
  545.0 75.1 %reduce-scatter.39.cloned.1.call-done = bf16[1,22,2048]{2,1,0:T(8,128)(2,1)} async-done(((bf16[16,22,2048]{2,1,0:T(8,128)(2,1)}), bf16[1,22,2048]{2,1,0:T(8,128)(2,1)}) %reduce-scatter.39.cloned.1.call-update) | async-done | bytes 90128
  620.1 0.9 convert_bitcast_fusion.10
  621.2 4.4 dynamic-update-slice.11
  625.5 4.4 dynamic-update-slice.12
  629.9 4.3 dynamic-update-slice.13
  634.2 21.5 %fusion.13 = (f32[1,299056]{1,0:T(1,128)}, f32[299056]{0:T(1024)}, f32[1,299056]{1,0:T(1,128)}, f32[299056]{0:T(1024)}) fusion(f32[1,299056]{1,0:T(1,128)} %dynamic-update-slice.13, f32[1,299056]{1,0:T(1,128)} %param.27, f32[1,299056]{1,0:T(1,128)} %param.26), kind=kLoop, calls=%fused_computation.30 | loop fusion | flops 2093392 | bytes 8373568 | tf_op jit(solution)/shard_map/add | solution.py:134
  655.8 16.2 %concatenate.41 = f32[299056]{0:T(1024)} concatenate(f32[16]{0:T(128)S(1)} %bitcast.103, f32[32768]{0:T(1024)S(1)} %bitcast.93, f32[32768]{0:T(1024)S(1)} %bitcast.94, f32[32768]{0:T(1024)S(1)} %bitcast.95, f32[16]{0:T(128)S(1)} %fusion.32, f32[32768]{0:T(1024)} %bitcast.96, f32[32768]{0:T(1024)} %bitcast.97, f32[16]{0:T(128)S(1)} %bitcast.104, f32[45056]{0:T(1024)S(1)} %reshape.617, ...), dimensions={0} | concatenate | bytes 2392448 | tf_op jit(solution)/shard_map/concatenate | solution.py:132
  672.0 4.2 fusion.24
  676.2 5.7 reshape.666
  682.0 12.5 %fusion.17 = f32[11]{0:T(128)S(1)} fusion(f32[299056,1]{0,1:T(1,128)S(1)} %reshape.666, s32[299056]{0:T(1024)S(1)} %convert_add_fusion), kind=kOutput, calls=%fused_computation.37 | convolution fusion | flops 42765008 | bytes 2392492 | tf_op jit(solution)/shard_map/dot_general | solution.py:10
  694.4 5.8 reshape.664
  700.3 12.5 %fusion.16 = f32[11]{0:T(128)S(1)} fusion(f32[299056,1]{0,1:T(1,128)S(1)} %reshape.664, s32[299056]{0:T(1024)S(1)} %convert_add_fusion), kind=kOutput, calls=%fused_computation.36 | convolution fusion | flops 42765008 | bytes 2392492 | tf_op jit(solution)/shard_map/dot_general | solution.py:10
  712.7 13.0 %all-reduce.15 = (f32[11]{0:T(128)S(1)}, f32[11]{0:T(128)S(1)}) all-reduce(f32[11]{0:T(128)S(1)} %fusion.17, f32[11]{0:T(128)S(1)} %fusion.16), channel_id=1, replica_groups=mesh['dp'=16,'tensor'=8] {'tensor'}, use_global_device_ids=true, to_apply=%region_13.0 | all-reduce | flops 22 | bytes 176 | tf_op jit(solution)/shard_map/psum | solution.py:137
  725.7 38.3 %all-reduce.14 = (f32[11]{0:T(128)S(1)}, f32[11]{0:T(128)S(1)}) all-reduce(f32[11]{0:T(128)S(1)} %get-tuple-element.30, f32[11]{0:T(128)S(1)} %get-tuple-element.31), channel_id=1, replica_groups=mesh['dp'=16,'tensor'=8] {'dp'}, use_global_device_ids=true, to_apply=%region_14.0 | all-reduce | flops 22 | bytes 176 | tf_op jit(solution)/shard_map/psum | solution.py:136
  764.1 20.0 %fusion.7 = f32[299056]{0:T(1024)S(1)} fusion(s32[299056]{0:T(1024)S(1)} %convert_add_fusion, f32[11]{0:T(128)S(1)} %get-tuple-element.28, f32[11]{0:T(128)S(1)} %get-tuple-element.29), kind=kOutput, calls=%fused_computation.22 | convolution fusion | flops 42765020 | bytes 2392536 | tf_op jit(solution)/shard_map/dot_general | solution.py:144
  788.5 0.7 copy.46
  789.5 0.7 copy.48
  791.7 6.6 reshape.620
  799.0 36.1 %all-reduce.16 = (bf16[256]{0:T(256)(128)(2,1)}, bf16[256]{0:T(256)(128)(2,1)}, bf16[256]{0:T(256)(128)(2,1)}) all-reduce(bf16[256]{0:T(256)(128)(2,1)S(1)} %dynamic-update-slice, bf16[256]{0:T(256)(128)(2,1)S(1)} %dynamic-update-slice.1, bf16[256]{0:T(256)(128)(2,1)S(1)} %dynamic-update-slice.2), channel_id=2, replica_groups=mesh['dp'=16,'tensor'=8] {'dp'}, use_global_device_ids=true, to_apply=%add | all-reduce | flops 768 | bytes 3072
  835.1 31.8 %all-gather.14.cloned.1.call-done = bf16[16,128,256]{2,1,0:T(8,128)(2,1)} async-done(((bf16[1,128,256]{2,1,0:T(8,128)(2,1)}), bf16[16,128,256]{2,1,0:T(8,128)(2,1)}) %all-gather.14.cloned.1.call-update) | async-done | bytes 1048592 | tf_op jit(solution)/shard_map/all_gather | solution.py:157
  867.0 45.1 %all-gather.16.cloned.1.call-done = bf16[16,128,256]{2,1,0:T(8,128)(2,1)} async-done(((bf16[1,128,256]{2,1,0:T(8,128)(2,1)}), bf16[16,128,256]{2,1,0:T(8,128)(2,1)}) %all-gather.16.cloned.1.call-update) | async-done | bytes 1048592 | tf_op jit(solution)/shard_map/all_gather | solution.py:158
  912.0 44.9 %all-gather.18.cloned.1.call-done = bf16[16,128,256]{2,1,0:T(8,128)(2,1)} async-done(((bf16[1,128,256]{2,1,0:T(8,128)(2,1)}), bf16[16,128,256]{2,1,0:T(8,128)(2,1)}) %all-gather.18.cloned.1.call-update) | async-done | bytes 1048592 | tf_op jit(solution)/shard_map/all_gather | solution.py:160
  957.0 45.1 %all-gather.20.cloned.1.call-done = bf16[16,16,2048]{2,1,0:T(8,128)(2,1)} async-done(((bf16[1,16,2048]{2,1,0:T(8,128)(2,1)}), bf16[16,16,2048]{2,1,0:T(8,128)(2,1)}) %all-gather.20.cloned.1.call-update) | async-done | bytes 1048592 | tf_op jit(solution)/shard_map/all_gather | solution.py:161
  1002.0 46.1 %all-gather.22.cloned.1.call-done = bf16[16,128,352]{1,2,0:T(8,128)(2,1)} async-done(((bf16[1,128,352]{1,2,0:T(8,128)(2,1)}), bf16[16,128,352]{1,2,0:T(8,128)(2,1)}) %all-gather.22.cloned.1.call-update) | async-done | bytes 1441808 | tf_op jit(solution)/shard_map/all_gather | solution.py:163
  1048.1 2.6 copy_bitcast_fusion.1
  1050.8 43.5 %all-gather.24.cloned.1.call-done = bf16[16,128,352]{1,2,0:T(8,128)(2,1)} async-done(((bf16[1,128,352]{1,2,0:T(8,128)(2,1)}), bf16[16,128,352]{1,2,0:T(8,128)(2,1)}) %all-gather.24.cloned.1.call-update) | async-done | bytes 1441808 | tf_op jit(solution)/shard_map/all_gather | solution.py:164
  1094.2 2.6 copy_bitcast_fusion
  1096.9 43.6 %all-gather.26.cloned.1.call-done = bf16[16,22,2048]{2,1,0:T(8,128)(2,1)} async-done(((bf16[1,22,2048]{2,1,0:T(8,128)(2,1)}), bf16[16,22,2048]{2,1,0:T(8,128)(2,1)}) %all-gather.26.cloned.1.call-update) | async-done | bytes 1441808 | tf_op jit(solution)/shard_map/all_gather | solution.py:165
  1140.4 2.4 reshape.642
  1142.9 1.0 copy.86
  1144.5 1.0 copy.87
  1146.1 1.0 copy.88
  1147.7 1.0 copy.89
  1149.3 1.0 copy.90
  (116 shorter events, 20.7 us)
Async XLA Ops:
  7.2 133.8 %reduce-scatter.25.cloned.1.call-start = ((), (), s32[]{:S(2)}) async-start(), calls=%async_computation.16 | async-start | bytes 1114112
  7.9 154.8 %reduce-scatter.27.cloned.1.call-start = ((), (), s32[]{:S(2)}) async-start(), calls=%async_computation.17 | async-start | bytes 1114112
  8.7 229.6 %reduce-scatter.29.cloned.1.call-start = ((), (), s32[]{:S(2)}) async-start(), calls=%async_computation.18 | async-start | bytes 1114112
  9.4 1.4 copy-start.1
  9.4 304.6 %reduce-scatter.31.cloned.1.call-start = ((), (), s32[]{:S(2)}) async-start(), calls=%async_computation.19 | async-start | bytes 1114112
  10.0 379.5 %reduce-scatter.33.cloned.1.call-start = ((), (), s32[]{:S(2)}) async-start(), calls=%async_computation.20 | async-start | bytes 1114112
  10.6 455.9 %reduce-scatter.35.cloned.1.call-start = ((), (), s32[]{:S(2)}) async-start(), calls=%async_computation.21 | async-start | bytes 1531904
  12.6 1.4 copy-start.2
  12.6 530.9 %reduce-scatter.37.cloned.1.call-start = ((), (), s32[]{:S(2)}) async-start(), calls=%async_computation.22 | async-start | bytes 1531904
  15.8 1.4 copy-start.3
  15.8 604.2 %reduce-scatter.39.cloned.1.call-start = ((), (), s32[]{:S(2)}) async-start(), calls=%async_computation.23 | async-start | bytes 1671168
  18.5 816.6 %all-gather.12.cloned.1.call-start = ((), (), s32[]{:S(2)}) async-start(), calls=%async_computation.8 | async-start | bytes 1114112 | tf_op jit(solution)/shard_map/all_gather | solution.py:156
  18.7 8.6 copy-start.15
  18.7 8.7 copy-start.16
  18.7 8.8 copy-start.17
  27.7 89.5 %copy-start.14 = (u32[128]{0:T(128)S(1)}, u32[128]{0:T(128)}, u32[]{:S(2)}) copy-start(u32[128]{0:T(128)} %constant.50) | copy-start | bytes 1540
  389.5 1.9 copy-start.11
  389.5 2.6 copy-start.12
  634.2 21.5 %copy-start.13 = (bf16[1,22,2048]{2,1,0:T(8,128)(2,1)S(1)}, bf16[1,22,2048]{2,1,0:T(8,128)(2,1)}, u32[]{:S(2)}) copy-start(bf16[1,22,2048]{2,1,0:T(8,128)(2,1)} %reduce-scatter.39.cloned.1.call-done) | copy-start | bytes 270340
  634.2 21.6 %copy-start.9 = (f32[16,2,8,128]{3,1,2,0:T(2,128)S(1)}, f32[16,2,8,128]{3,1,2,0:T(2,128)}, u32[]{:S(2)}) copy-start(f32[16,2,8,128]{3,1,2,0:T(2,128)} %copy.53) | copy-start | bytes 393220
  634.2 21.6 %copy-start.10 = (f32[16,2,8,128]{3,1,2,0:T(2,128)S(1)}, f32[16,2,8,128]{3,1,2,0:T(2,128)}, u32[]{:S(2)}) copy-start(f32[16,2,8,128]{3,1,2,0:T(2,128)} %copy.54) | copy-start | bytes 393220
  764.1 20.0 %copy-start = (f32[299056]{0:T(1024)S(1)}, f32[299056]{0:T(1024)}, u32[]{:S(2)}) copy-start(f32[299056]{0:T(1024)} %get-tuple-element.41) | copy-start | bytes 3588676
  785.2 81.8 %all-gather.14.cloned.1.call-start = ((), (), s32[]{:S(2)}) async-start(), calls=%async_computation.9 | async-start | bytes 1114112 | tf_op jit(solution)/shard_map/all_gather | solution.py:157
  785.9 126.1 %all-gather.16.cloned.1.call-start = ((), (), s32[]{:S(2)}) async-start(), calls=%async_computation.10 | async-start | bytes 1114112 | tf_op jit(solution)/shard_map/all_gather | solution.py:158
  786.7 170.3 %all-gather.18.cloned.1.call-start = ((), (), s32[]{:S(2)}) async-start(), calls=%async_computation.11 | async-start | bytes 1114112 | tf_op jit(solution)/shard_map/all_gather | solution.py:160
  787.4 214.6 %all-gather.20.cloned.1.call-start = ((), (), s32[]{:S(2)}) async-start(), calls=%async_computation.12 | async-start | bytes 1114112 | tf_op jit(solution)/shard_map/all_gather | solution.py:161
  788.1 260.0 %all-gather.22.cloned.1.call-start = ((), (), s32[]{:S(2)}) async-start(), calls=%async_computation.13 | async-start | bytes 1531904 | tf_op jit(solution)/shard_map/all_gather | solution.py:163
  789.3 304.9 %all-gather.24.cloned.1.call-start = ((), (), s32[]{:S(2)}) async-start(), calls=%async_computation.14 | async-start | bytes 1531904 | tf_op jit(solution)/shard_map/all_gather | solution.py:164
  790.3 350.2 %all-gather.26.cloned.1.call-start = ((), (), s32[]{:S(2)}) async-start(), calls=%async_computation.15 | async-start | bytes 1671168 | tf_op jit(solution)/shard_map/all_gather | solution.py:165
  1096.9 46.0 %copy-start.4 = (bf16[16,128,256]{2,1,0:T(8,128)(2,1)S(1)}, bf16[16,128,256]{2,1,0:T(8,128)(2,1)}, u32[]{:S(2)}) copy-start(bf16[16,128,256]{2,1,0:T(8,128)(2,1)} %all-gather.12.cloned.1.call-done) | copy-start | bytes 3145732
  1142.9 1.6 copy-start.5
  1144.5 1.6 copy-start.6
  1146.1 1.6 copy-start.7
  1147.7 1.6 copy-start.8
Sparse Core Ops, SparseCore 0:
  11.2 75.6 reduce-scatter.24
  90.4 72.2 reduce-scatter.26
  165.9 72.2 reduce-scatter.28
  241.7 72.2 reduce-scatter.30
  317.0 72.3 reduce-scatter.32
  393.4 72.9 reduce-scatter.34
  470.6 72.9 reduce-scatter.36
  547.1 72.9 reduce-scatter.38
  785.3 36.6 all-gather.11
  824.8 42.0 all-gather.13
  869.9 42.0 all-gather.15
  914.8 42.0 all-gather.17
  959.9 42.0 all-gather.19
  1004.9 43.1 all-gather.21
  1050.9 43.2 all-gather.23
  1097.1 43.3 all-gather.25
